TPU v7x, 512 devices: a whole 4x4x16 slice. The times are simulated.
512 devices in a mesh: loop: 64 (over y_lo, z, core), grp: 8 (over x, y_hi).
Axes of the slice: x: 4, y: 4 (y_hi: 2, y_lo: 2; y = y_hi * 2 + y_lo), z: 16, core: 2. Of those that a mesh axis runs over, the one named last changes fastest.
Arguments:
- ratings: bfloat16 [2, 262144, 2048], P(None, ('loop', 'grp')), may hold values from -2.5 to 2.5, as said below
- user_factors: float32 [262144, 128], P(('loop', 'grp')), may hold values from -2 to 2
- user_accum: float32 [262144, 128], P(('loop', 'grp')), may hold values from 20 to 400
- item_factors: float32 [131072, 128], P('loop'), may hold values from -2 to 2
- item_accum: float32 [131072, 128], P('loop'), may hold values from 20 to 400
Outputs:
- users_out: float32 [262144, 128], P(('loop', 'grp'))
- items_out: float32 [131072, 128], P('loop')
Inputs may be any that keep to these rules, and one draw needn't show every extreme that they name: `ratings`: each entry is 0 (unobserved) or has magnitude 0.5 or more.
All inputs are finite; a program needn't handle non-finite values.
Results may differ from a plain program's by a relative error of at most 0.0085.
Values may be sent and summed in bfloat16 or wider, within the bound.
A program may use at most 64 MiB of HBM per device.

v0:
```python
import jax
import jax.numpy as jnp
from jax import lax
from jax.sharding import PartitionSpec as P

SUB = 2
INNER = 2
shrink = 0.05
learn_rate = 0.2
tiny_eps = 1e-06


def shifted(shard, axis, by):
    devices = lax.axis_size(axis)
    return lax.ppermute(shard, axis, [(i, (i + by) % devices) for i in range(devices)])


def adagrad(param, accum, grad):
    accum = accum + grad * grad
    return (param - learn_rate * grad / jnp.sqrt(accum + tiny_eps), accum)


def residual_terms(rate_full, observed, users, item_half):
    user_half = users.astype(jnp.bfloat16)
    predicted = lax.dot_general(
        user_half, item_half, (((1,), (1,)), ((), ())), preferred_element_type=jnp.float32
    )
    resid = (observed * (rate_full - predicted)).astype(jnp.bfloat16)
    grad_user = -jnp.dot(resid, item_half, preferred_element_type=jnp.float32) + shrink * users
    return (user_half, resid, grad_user)


def local(ratings, user_factors, user_accum, item_factors, item_accum):
    users = user_factors
    user_acc = user_accum
    items = item_factors
    item_acc = item_accum
    for sub_epoch in range(SUB):
        if sub_epoch > 0:
            items, item_acc = shifted((items, item_acc), "loop", 1)
        rate_full = ratings[sub_epoch].astype(jnp.float32)
        observed = (jnp.abs(rate_full) > 0.25).astype(jnp.float32)
        for inner_step in range(INNER):
            item_half = items.astype(jnp.bfloat16)
            user_half, resid, grad_user = residual_terms(rate_full, observed, users, item_half)
            own_term = -lax.dot_general(
                resid, user_half, (((0,), (0,)), ((), ())), preferred_element_type=jnp.float32
            )
            grad_item = (
                lax.psum(own_term.astype(jnp.bfloat16), "grp").astype(jnp.float32) + shrink * items
            )
            users, user_acc = adagrad(users, user_acc, grad_user)
            items, item_acc = adagrad(items, item_acc, grad_item)
    return (users, items)


def solution(mesh):
    in_specs = (
        P(None, ("loop", "grp"), None),
        P(("loop", "grp"), None),
        P(("loop", "grp"), None),
        P("loop", None),
        P("loop", None),
    )
    out_specs = (P(("loop", "grp"), None), P("loop", None))
    return jax.shard_map(local, mesh=mesh, in_specs=in_specs, out_specs=out_specs, check_vma=False)
```

profile of v0, /device:TPU:32, one launch (start us, length us, event | category | flops | bytes accessed | tf_op | source)
XLA Modules:
  0.0 459.4 jit_solution(7370954499293579164)
XLA Ops:
  7.2 0.0 all-reduce.5.cloned.1.call-start
  7.2 0.0 copy-start.6
  7.2 3.0 fusion.2
  10.2 0.0 copy-done.6
  10.3 0.0 copy-start
  10.3 0.0 copy-start.5
  10.3 1.6 fusion.10
  11.8 0.0 all-reduce.5.cloned.1.call-update
  11.9 0.0 all-reduce.7.cloned.1.call-start
  11.9 0.0 copy-done
  11.9 0.0 copy-done.5
  11.9 2.5 multiply_subtract_fusion.7
  14.4 103.1 %all-reduce.5.cloned.1.call-done = bf16[2048,128]{1,0:T(8,128)(2,1)} async-done(((bf16[2048,128]{1,0:T(8,128)(2,1)}), bf16[2048,128]{1,0:T(8,128)(2,1)}) %all-reduce.5.cloned.1.call-update) | async-done | bytes 524304 | tf_op jit(solution)/shard_map/psum | solution.py:50
  117.5 0.0 copy-start.3
  117.5 3.4 fusion.4
  120.9 0.0 copy-done.3
  120.9 1.6 fusion.11
  122.5 0.0 all-reduce.7.cloned.1.call-update
  122.5 0.0 all-reduce.9.cloned.1.call-start
  122.5 99.3 %all-reduce.7.cloned.1.call-done = bf16[2048,128]{1,0:T(8,128)(2,1)} async-done(((bf16[2048,128]{1,0:T(8,128)(2,1)}), bf16[2048,128]{1,0:T(8,128)(2,1)}) %all-reduce.7.cloned.1.call-update) | async-done | bytes 524304 | tf_op jit(solution)/shard_map/psum | solution.py:50
  221.8 0.0 copy-start.1
  221.8 0.0 copy-start.2
  221.8 0.0 copy-start.4
  221.8 3.3 multiply_add_fusion.2
  225.1 1.9 collective-permute-start
  227.0 0.0 copy-done.1
  227.0 0.0 copy-done.2
  227.1 0.0 copy-done.4
  227.1 0.0 copy-start.8
  227.1 2.8 multiply_subtract_fusion.6
  229.9 3.6 collective-permute-start.1
  233.4 7.8 %collective-permute-done = f32[2048,128]{1,0:T(8,128)S(1)} collective-permute-done((f32[2048,128]{1,0:T(8,128)S(1)}, f32[2048,128]{1,0:T(8,128)S(1)}, u32[]{:S(2)}, u32[]{:S(2)}) %collective-permute-start) | collective-permute-done | bytes 1048608 | tf_op jit(solution)/shard_map/ppermute | solution.py:15
  241.2 0.0 copy-done.8
  241.2 1.0 fusion.7
  242.3 1.6 fusion.12
  243.8 0.0 all-reduce.9.cloned.1.call-update
  243.9 0.2 all-reduce.11.cloned.1.call-start
  244.1 2.4 fusion.25
  246.5 6.1 %collective-permute-done.1 = f32[2048,128]{1,0:T(8,128)} collective-permute-done((f32[2048,128]{1,0:T(8,128)}, f32[2048,128]{1,0:T(8,128)}, u32[]{:S(2)}, u32[]{:S(2)}) %collective-permute-start.1) | collective-permute-done | bytes 1048608 | tf_op jit(solution)/shard_map/ppermute | solution.py:15
  252.6 91.8 %all-reduce.9.cloned.1.call-done = bf16[2048,128]{1,0:T(8,128)(2,1)} async-done(((bf16[2048,128]{1,0:T(8,128)(2,1)}), bf16[2048,128]{1,0:T(8,128)(2,1)}) %all-reduce.9.cloned.1.call-update) | async-done | bytes 524304 | tf_op jit(solution)/shard_map/psum | solution.py:50
  344.4 1.7 fusion.18
  346.1 0.0 copy-start.7
  346.1 2.7 fusion.9
  348.8 0.0 copy-done.7
  348.9 1.6 fusion.13
  350.4 0.0 all-reduce.11.cloned.1.call-update
  350.5 2.6 multiply_subtract_fusion.4
  353.1 96.6 %all-reduce.11.cloned.1.call-done = bf16[2048,128]{1,0:T(8,128)(2,1)} async-done(((bf16[2048,128]{1,0:T(8,128)(2,1)}), bf16[2048,128]{1,0:T(8,128)(2,1)}) %all-reduce.11.cloned.1.call-update) | async-done | bytes 524304 | tf_op jit(solution)/shard_map/psum | solution.py:50
  449.7 3.2 multiply_subtract_fusion
Async XLA Ops:
  7.2 110.3 %all-reduce.5.cloned.1.call-start = ((), (), s32[]{:S(2)}) async-start(), calls=%async_computation | async-start | bytes 1048576 | tf_op jit(solution)/shard_map/psum | solution.py:50
  7.2 3.0 copy-start.6
  10.3 1.7 copy-start
  10.3 1.7 copy-start.5
  11.9 209.9 %all-reduce.7.cloned.1.call-start = ((), (), s32[]{:S(2)}) async-start(), calls=%async_computation.1 | async-start | bytes 1048576 | tf_op jit(solution)/shard_map/psum | solution.py:50
  117.5 3.4 copy-start.3
  122.5 221.9 %all-reduce.9.cloned.1.call-start = ((), (), s32[]{:S(2)}) async-start(), calls=%async_computation.2 | async-start | bytes 1048576 | tf_op jit(solution)/shard_map/psum | solution.py:50
  221.8 5.2 %copy-start.1 = (f32[2048,128]{1,0:T(8,128)S(1)}, f32[2048,128]{1,0:T(8,128)}, u32[]{:S(2)}) copy-start(f32[2048,128]{1,0:T(8,128)} %param.8) | copy-start | bytes 3145732
  221.8 5.2 %copy-start.2 = (f32[2048,128]{1,0:T(8,128)S(1)}, f32[2048,128]{1,0:T(8,128)}, u32[]{:S(2)}) copy-start(f32[2048,128]{1,0:T(8,128)} %param.9) | copy-start | bytes 3145732
  221.8 5.3 %copy-start.4 = (bf16[2048,128]{1,0:T(8,128)(2,1)S(1)}, bf16[2048,128]{1,0:T(8,128)(2,1)}, u32[]{:S(2)}) copy-start(bf16[2048,128]{1,0:T(8,128)(2,1)} %all-reduce.5.cloned.1.call-done) | copy-start | bytes 1572868
  225.1 16.1 %collective-permute-start = (f32[2048,128]{1,0:T(8,128)S(1)}, f32[2048,128]{1,0:T(8,128)S(1)}, u32[]{:S(2)}, u32[]{:S(2)}) collective-permute-start(f32[2048,128]{1,0:T(8,128)S(1)} %get-tuple-element.5), channel_id=1, source_target_pairs={{0,8},{8,16},{16,24},{24,32},{32,40},{40,48},{48,56},{56,64},{64,7... | collective-permute-start | bytes 3145736 | tf_op jit(solution)/shard_map/ppermute | solution.py:15
  227.1 14.2 %copy-start.8 = (bf16[2,512,2048]{2,1,0:T(8,128)(2,1)S(1)}, bf16[2,512,2048]{2,1,0:T(8,128)(2,1)}, u32[]{:S(2)}) copy-start(bf16[2,512,2048]{2,1,0:T(8,128)(2,1)} %param.5) | copy-start | bytes 12582916
  229.9 22.7 %collective-permute-start.1 = (f32[2048,128]{1,0:T(8,128)}, f32[2048,128]{1,0:T(8,128)}, u32[]{:S(2)}, u32[]{:S(2)}) collective-permute-start(f32[2048,128]{1,0:T(8,128)} %get-tuple-element.4), channel_id=1, source_target_pairs={{0,8},{8,16},{16,24},{24,32},{32,40},{40,48},{48,56},{56,64},{64,7... | collective-permute-start | bytes 3145736 | tf_op jit(solution)/shard_map/ppermute | solution.py:15
  243.9 205.9 %all-reduce.11.cloned.1.call-start = ((), (), s32[]{:S(2)}) async-start(), calls=%async_computation.3 | async-start | bytes 1048576 | tf_op jit(solution)/shard_map/psum | solution.py:50
  346.1 2.7 copy-start.7
Sparse Core Ops, SparseCore 0:
  12.0 105.4 all-reduce.4
  122.6 99.1 all-reduce.6
  244.0 100.3 all-reduce.8
  350.6 99.0 all-reduce.10
where the time goes:
time: 460 us; the launch traced here: 459 us
  waiting for transfers between devices  405 us (88%)
  matrix products  26.7 us (6%)
  between operations  13.9 us (3%)
  other arithmetic  8.22 us (2%)
  starting transfers between devices  5.81 us (1%)
    psum x4, waiting for transfers between devices, local(): lax.psum(own_term.astype(jnp.bfloat16), 'grp').astype(jnp.float32)  391 us
    ppermute x2, waiting for transfers between devices, shifted(): lax.ppermute(shard, axis, [(i, (i + by) % devices) for i in range(devices)])  13.9 us
    dot_general x4, matrix products, residual_terms(): jnp.dot(resid, item_half, preferred_element_type=jnp.float32)  10.3 us
    dot_general x4, matrix products, residual_terms(): lax.dot_general(user_half, item_half, (((1,), (1,)), ((), ())), preferred...  10.2 us
  transfers between devices with their start and end apart: 6, of which 6 were waited for; matrix products, arithmetic and copies ran while one was open for 3% of the time, Pallas kernels for 0%

commit v1 on v0

--- a/solution.py
+++ b/solution.py
@@ -8,6 +8,10 @@
 shrink = 0.05
 learn_rate = 0.2
 tiny_eps = 1e-06
+
+
+def _move_sheet(u_in):
+    return lax.all_gather(u_in, axis_name="grp").sum(axis=0)
 
 
 def shifted(shard, axis, by):
@@ -47,7 +51,7 @@
                 resid, user_half, (((0,), (0,)), ((), ())), preferred_element_type=jnp.float32
             )
             grad_item = (
-                lax.psum(own_term.astype(jnp.bfloat16), "grp").astype(jnp.float32) + shrink * items
+                _move_sheet(own_term.astype(jnp.bfloat16)).astype(jnp.float32) + shrink * items
             )
             users, user_acc = adagrad(users, user_acc, grad_user)
             items, item_acc = adagrad(items, item_acc, grad_item)

time: 460 us -> 418 us (0.909)
  the two profiles are of different devices: /device:TPU:32 before, /device:TPU:1 now
where the time goes in v1:
time: 418 us; the launch traced here: 417 us
  waiting for transfers between devices  346 us (83%)
  matrix products  25.1 us (6%)
  other arithmetic  21.5 us (5%)
  between operations  14 us (3%)
  starting transfers between devices  9.45 us (2%)
    all_gather x4, waiting for transfers between devices, _move_sheet(): return lax.all_gather(u_in, axis_name='grp').sum(axis=0)  336 us
    reduce_sum x4, other arithmetic, _move_sheet(): return lax.all_gather(u_in, axis_name='grp').sum(axis=0)  13.5 us
    ppermute x2, waiting for transfers between devices, shifted(): lax.ppermute(shard, axis, [(i, (i + by) % devices) for i in range(devices)])  10.1 us
    dot_general x4, matrix products, residual_terms(): lax.dot_general(user_half, item_half, (((1,), (1,)), ((), ())), preferred...  9.87 us
    ppermute x2, starting transfers between devices, shifted(): lax.ppermute(shard, axis, [(i, (i + by) % devices) for i in range(devices)])  9.29 us
    dot_general x4, matrix products, residual_terms(): jnp.dot(resid, item_half, preferred_element_type=jnp.float32)  8.98 us
  transfers between devices with their start and end apart: 6, of which 5 were waited for; matrix products, arithmetic and copies ran while one was open for 3% of the time, Pallas kernels for 0%

profile of v1, /device:TPU:1, one launch (start us, length us, event | category | flops | bytes accessed | tf_op | source)
XLA Modules:
  0.0 417.1 jit_solution(15496833185395703203)
XLA Ops:
  7.2 0.0 copy-start.10
  7.2 0.0 all-gather.9.cloned.1.call-start
  7.2 3.0 fusion.2
  10.2 0.0 copy-done.10
  10.2 0.0 copy-start
  10.3 1.6 fusion.10
  11.8 0.0 all-gather.9.cloned.1.call-update
  11.8 0.0 all-gather.11.cloned.1.call-start
  11.9 0.0 copy-done
  11.9 2.4 multiply_subtract_fusion.7
  14.4 0.0 copy-start.6
  14.4 89.2 %all-gather.9.cloned.1.call-done = bf16[16384,128]{1,0:T(8,128)(2,1)} async-done(((bf16[2048,128]{1,0:T(8,128)(2,1)}), bf16[16384,128]{1,0:T(8,128)(2,1)}) %all-gather.9.cloned.1.call-update) | async-done | bytes 4194320 | tf_op jit(solution)/shard_map/all_gather | solution.py:14
  103.6 3.7 reduce_sum.48
  107.3 3.3 fusion.4
  110.6 0.0 copy-done.6
  110.6 1.6 fusion.11
  112.1 0.0 all-gather.11.cloned.1.call-update
  112.2 0.0 all-gather.13.cloned.1.call-start
  112.2 85.1 %all-gather.11.cloned.1.call-done = bf16[16384,128]{1,0:T(8,128)(2,1)} async-done(((bf16[2048,128]{1,0:T(8,128)(2,1)}), bf16[16384,128]{1,0:T(8,128)(2,1)}) %all-gather.11.cloned.1.call-update) | async-done | bytes 4194320 | tf_op jit(solution)/shard_map/all_gather | solution.py:14
  197.3 3.7 reduce_sum.49
  201.0 0.0 copy-start.1
  201.0 0.0 copy-start.4
  201.0 0.0 copy-start.5
  201.0 0.0 copy-start.7
  201.0 0.0 copy-start.8
  201.0 0.0 copy-start.9
  201.0 3.3 multiply_add_fusion.2
  204.3 0.0 copy-start.12
  204.3 4.7 %collective-permute-start = (f32[2048,128]{1,0:T(8,128)S(1)}, f32[2048,128]{1,0:T(8,128)S(1)}, u32[]{:S(2)}, u32[]{:S(2)}) collective-permute-start(f32[2048,128]{1,0:T(8,128)S(1)} %get-tuple-element.5), channel_id=1, source_target_pairs={{0,8},{8,16},{16,24},{24,32},{32,40},{40,48},{48,56},{56,64},{64,7... | collective-permute-start | bytes 3145736 | tf_op jit(solution)/shard_map/ppermute | solution.py:19
  209.1 0.0 copy-done.1
  209.1 0.0 copy-done.4
  209.1 0.0 copy-done.5
  209.1 0.0 copy-done.7
  209.1 0.0 copy-done.8
  209.1 0.0 copy-done.9
  209.1 1.5 multiply_subtract_fusion.6
  210.6 10.1 %collective-permute-done = f32[2048,128]{1,0:T(8,128)S(1)} collective-permute-done((f32[2048,128]{1,0:T(8,128)S(1)}, f32[2048,128]{1,0:T(8,128)S(1)}, u32[]{:S(2)}, u32[]{:S(2)}) %collective-permute-start) | collective-permute-done | bytes 1048608 | tf_op jit(solution)/shard_map/ppermute | solution.py:19
  220.8 0.0 copy-done.12
  220.8 1.0 fusion.7
  221.8 1.6 fusion.12
  223.4 0.0 all-gather.13.cloned.1.call-update
  223.4 0.0 all-gather.15.cloned.1.call-start
  223.5 4.6 %collective-permute-start.1 = (f32[2048,128]{1,0:T(8,128)}, f32[2048,128]{1,0:T(8,128)}, u32[]{:S(2)}, u32[]{:S(2)}) collective-permute-start(f32[2048,128]{1,0:T(8,128)} %get-tuple-element.4), channel_id=1, source_target_pairs={{0,8},{8,16},{16,24},{24,32},{32,40},{40,48},{48,56},{56,64},{64,7... | collective-permute-start | bytes 3145736 | tf_op jit(solution)/shard_map/ppermute | solution.py:19
  228.1 2.4 fusion.25
  230.4 79.3 %all-gather.13.cloned.1.call-done = bf16[16384,128]{1,0:T(8,128)(2,1)} async-done(((bf16[2048,128]{1,0:T(8,128)(2,1)}), bf16[16384,128]{1,0:T(8,128)(2,1)}) %all-gather.13.cloned.1.call-update) | async-done | bytes 4194320 | tf_op jit(solution)/shard_map/all_gather | solution.py:14
  309.7 3.1 reduce_sum.50
  312.8 0.0 copy-start.2
  312.8 0.0 collective-permute-done.1
  312.8 1.8 fusion.18
  314.6 0.0 copy-done.2
  314.6 0.0 copy-start.11
  314.6 0.8 copy-done.11
  315.4 2.5 fusion.9
  317.9 1.6 fusion.13
  319.5 0.0 all-gather.15.cloned.1.call-update
  319.5 2.6 multiply_subtract_fusion.4
  322.1 0.0 copy-start.3
  322.1 82.5 %all-gather.15.cloned.1.call-done = bf16[16384,128]{1,0:T(8,128)(2,1)} async-done(((bf16[2048,128]{1,0:T(8,128)(2,1)}), bf16[16384,128]{1,0:T(8,128)(2,1)}) %all-gather.15.cloned.1.call-update) | async-done | bytes 4194320 | tf_op jit(solution)/shard_map/all_gather | solution.py:14
  404.6 3.1 reduce_sum.51
  407.7 0.0 copy-done.3
  407.7 2.9 multiply_subtract_fusion
Async XLA Ops:
  7.2 3.1 copy-start.10
  7.2 96.4 %all-gather.9.cloned.1.call-start = ((), (), s32[]{:S(2)}) async-start(), calls=%async_computation | async-start | bytes 4718592 | tf_op jit(solution)/shard_map/all_gather | solution.py:14
  10.2 1.7 copy-start
  11.8 185.4 %all-gather.11.cloned.1.call-start = ((), (), s32[]{:S(2)}) async-start(), calls=%async_computation.1 | async-start | bytes 4718592 | tf_op jit(solution)/shard_map/all_gather | solution.py:14
  14.4 96.2 %copy-start.6 = (f32[512,128]{1,0:T(8,128)}, f32[512,128]{1,0:T(8,128)S(1)}, u32[]{:S(2)}) copy-start(f32[512,128]{1,0:T(8,128)S(1)} %get-tuple-element.6) | copy-start | bytes 786436
  112.2 197.6 %all-gather.13.cloned.1.call-start = ((), (), s32[]{:S(2)}) async-start(), calls=%async_computation.2 | async-start | bytes 4718592 | tf_op jit(solution)/shard_map/all_gather | solution.py:14
  201.0 8.1 %copy-start.1 = (f32[2048,128]{1,0:T(8,128)S(1)}, f32[2048,128]{1,0:T(8,128)}, u32[]{:S(2)}) copy-start(f32[2048,128]{1,0:T(8,128)} %param.8) | copy-start | bytes 3145732
  201.0 8.1 %copy-start.4 = (bf16[2048,128]{1,0:T(8,128)(2,1)S(1)}, bf16[2048,128]{1,0:T(8,128)(2,1)}, u32[]{:S(2)}) copy-start(bf16[2048,128]{1,0:T(8,128)(2,1)} %reduce_sum.48) | copy-start | bytes 1572868
  201.0 8.1 %copy-start.5 = (f32[2048,128]{1,0:T(8,128)S(1)}, f32[2048,128]{1,0:T(8,128)}, u32[]{:S(2)}) copy-start(f32[2048,128]{1,0:T(8,128)} %param.9) | copy-start | bytes 3145732
  201.0 8.1 %copy-start.7 = (f32[512,128]{1,0:T(8,128)S(1)}, f32[512,128]{1,0:T(8,128)}, u32[]{:S(2)}) copy-start(f32[512,128]{1,0:T(8,128)} %copy-done.6) | copy-start | bytes 786436
  201.0 8.1 %copy-start.8 = (f32[512,128]{1,0:T(8,128)S(1)}, f32[512,128]{1,0:T(8,128)}, u32[]{:S(2)}) copy-start(f32[512,128]{1,0:T(8,128)} %param.7) | copy-start | bytes 786436
  201.0 8.1 %copy-start.9 = (f32[512,128]{1,0:T(8,128)S(1)}, f32[512,128]{1,0:T(8,128)}, u32[]{:S(2)}) copy-start(f32[512,128]{1,0:T(8,128)} %get-tuple-element.7) | copy-start | bytes 786436
  204.3 16.5 %copy-start.12 = (bf16[2,512,2048]{2,1,0:T(8,128)(2,1)S(1)}, bf16[2,512,2048]{2,1,0:T(8,128)(2,1)}, u32[]{:S(2)}) copy-start(bf16[2,512,2048]{2,1,0:T(8,128)(2,1)} %param.5) | copy-start | bytes 12582916
  204.3 16.4 %collective-permute-start = (f32[2048,128]{1,0:T(8,128)S(1)}, f32[2048,128]{1,0:T(8,128)S(1)}, u32[]{:S(2)}, u32[]{:S(2)}) collective-permute-start(f32[2048,128]{1,0:T(8,128)S(1)} %get-tuple-element.5), channel_id=1, source_target_pairs={{0,8},{8,16},{16,24},{24,32},{32,40},{40,48},{48,56},{56,64},{64,7... | collective-permute-start | bytes 3145736 | tf_op jit(solution)/shard_map/ppermute | solution.py:19
  223.4 181.2 %all-gather.15.cloned.1.call-start = ((), (), s32[]{:S(2)}) async-start(), calls=%async_computation.3 | async-start | bytes 4718592 | tf_op jit(solution)/shard_map/all_gather | solution.py:14
  223.5 89.3 %collective-permute-start.1 = (f32[2048,128]{1,0:T(8,128)}, f32[2048,128]{1,0:T(8,128)}, u32[]{:S(2)}, u32[]{:S(2)}) collective-permute-start(f32[2048,128]{1,0:T(8,128)} %get-tuple-element.4), channel_id=1, source_target_pairs={{0,8},{8,16},{16,24},{24,32},{32,40},{40,48},{48,56},{56,64},{64,7... | collective-permute-start | bytes 3145736 | tf_op jit(solution)/shard_map/ppermute | solution.py:19
  312.8 1.8 copy-start.2
  314.6 0.8 copy-start.11
  322.1 85.6 %copy-start.3 = (bf16[2048,128]{1,0:T(8,128)(2,1)S(1)}, bf16[2048,128]{1,0:T(8,128)(2,1)}, u32[]{:S(2)}) copy-start(bf16[2048,128]{1,0:T(8,128)(2,1)} %copy-done.2) | copy-start | bytes 1572868
Sparse Core Ops, SparseCore 0:
  12.0 91.5 all-gather.8
  112.3 84.9 all-gather.10
  223.6 86.1 all-gather.12
  319.6 84.9 all-gather.14
